TPU v7x, 512 devices: a whole 4x8x8 slice. The times are simulated.
512 devices in a mesh: grp: 4 (over z_hi, core), wide: 128 (over z_lo, x, y).
Axes of the slice: x: 4, y: 8, z: 8 (z_hi: 2, z_lo: 4; z = z_hi * 4 + z_lo), core: 2. Of those that a mesh axis runs over, the one named last changes fastest.
Arguments:
- images: bfloat16 [2048, 256, 2048], P(('grp', 'wide')), may hold values from -6 to 6
- legendre_real: float32 [128, 128], replicated, may hold values from -0.375 to 0.375
- legendre_imag: float32 [128, 128], replicated, may hold values from -0.375 to 0.375
- amplitudes: float32 [128, 256, 128], P('wide'), may hold values from -6 to 6
Outputs:
- projected: float32 [128, 256, 128], P('wide', 'grp')
All inputs are finite; a program needn't handle non-finite values.
Results may differ from a plain program's by a relative error of at most 0.0023.
Values may be sent and summed in bfloat16 or wider, within the bound.
No kernel may reach another device: no remote copies, remote signals or barrier semaphores. Data moves between devices by JAX's collectives and lax.ppermute only.
A program may use at most 64 MiB of HBM per device.

v0:
```python
import math

import jax
import jax.numpy as jnp
from jax import lax
from jax.sharding import PartitionSpec as P

HARMS = 128


def harmonic_rows(points, count):
    angle_idx = jnp.arange(points, dtype=jnp.int32)
    harm_idx = jnp.arange(count, dtype=jnp.int32)
    product = harm_idx[:, None] * angle_idx[None, :] % points
    phase = product.astype(jnp.float32) * (2.0 * math.pi / points)
    norm_scale = 1.0 / math.sqrt(points)
    both = jnp.stack([jnp.cos(phase) * norm_scale, -jnp.sin(phase) * norm_scale], axis=1)
    return both.reshape(count * 2, points).astype(jnp.bfloat16)


def invert_harms(stacked, legendre_real, legendre_imag):
    result = jnp.dot(legendre_real, stacked[:, 0], precision=lax.Precision.HIGHEST)
    return result + jnp.dot(legendre_imag, stacked[:, 1], precision=lax.Precision.HIGHEST)


def body(images, legendre_real, legendre_imag, amplitudes):
    local_img, radii, points = images.shape
    table_rows = harmonic_rows(points, HARMS)
    flat_images = images.reshape(local_img * radii, points)
    spectra = lax.dot_general(
        table_rows, flat_images, (((1,), (1,)), ((), ())), preferred_element_type=jnp.float32
    )
    spectra = spectra.astype(jnp.bfloat16).reshape(HARMS, 2, local_img, radii)
    pooled = lax.all_to_all(spectra, "wide", split_axis=0, concat_axis=2, tiled=True)
    total_img = pooled.shape[2] * lax.axis_size("grp")
    gram = jnp.einsum("kanr,kbns->kabrs", pooled, pooled, preferred_element_type=jnp.float32)
    real_part = (gram[:, 0, 0] + gram[:, 1, 1]) / total_img
    imag_part = (gram[:, 1, 0] - gram[:, 0, 1]) / total_img
    corr = jnp.stack([real_part, imag_part], axis=1)
    own_harms = corr.shape[0]
    own_degrees = amplitudes.shape[0]
    groups = lax.axis_size("grp")
    summed = lax.psum_scatter(corr, "grp", scatter_dimension=2, tiled=True)
    flat = summed.reshape(own_harms, 2, radii // groups * radii)
    every_harm = lax.all_to_all(flat, "wide", split_axis=2, concat_axis=0, tiled=True)
    degree_part = invert_harms(every_harm, legendre_real, legendre_imag)
    mine = lax.all_to_all(degree_part, "wide", split_axis=0, concat_axis=1, tiled=True)
    inverted = mine.reshape(own_degrees, radii // groups, radii)
    return jnp.einsum("lrs,lsk->lrk", inverted, amplitudes, precision=lax.Precision.HIGHEST)


def solution(mesh):
    return jax.shard_map(
        body,
        mesh=mesh,
        in_specs=(P(("grp", "wide"), None, None), P(), P(), P("wide", None, None)),
        out_specs=P("wide", "grp", None),
        check_vma=False,
    )
```

profile of v0, /device:TPU:8, one launch (start us, length us, event | category | flops | bytes accessed | tf_op | source)
XLA Modules:
  0.0 285.0 jit_solution(9286189481164600383)
XLA Ops:
  6.5 0.0 copy-start
  6.5 0.0 all-reduce.3.cloned.1.call-start
  6.5 4.3 %multiply_convert_fusion = (bf16[128,1,2048]{2,0,1:T(8,128)(2,1)S(1)}, bf16[128,1,2048]{2,0,1:T(8,128)(2,1)S(1)}) fusion(), kind=kLoop, calls=%fused_computation.12 | loop fusion | flops 4980736 | bytes 1048576 | tf_op jit(solution)/shard_map/convert.1
  10.9 0.1 pad_maximum_fusion
  11.0 1.1 copy.43
  12.1 0.4 convert_element_type.30
  12.5 3.5 %convolution_convert_fusion = bf16[256,1024]{1,0:T(8,128)(2,1)S(1)} fusion(bf16[256,2048]{1,0:T(8,128)(2,1)S(1)} %convert_element_type.30, bf16[1024,2048]{1,0:T(8,128)(2,1)} %bitcast.73), kind=kOutput, calls=%fused_computation.4 | convolution fusion | flops 1074003968 | bytes 5767168 | tf_op jit(solution)/shard_map/dot_general | solution.py:30
  16.0 0.4 reshape.176
  16.4 37.3 %all_to_all.46 = bf16[128,2,4,256]{3,2,1,0:T(4,128)(2,1)S(1)} all-to-all(bf16[128,2,4,256]{3,2,1,0:T(4,128)(2,1)S(1)} %reshape.176), channel_id=1, replica_groups=mesh['grp'=4,'wide'=128] {'wide'}, dimensions={0} | all-to-all | bytes 1048576 | tf_op jit(solution)/shard_map/all_to_all | solution.py:34
  53.7 0.5 copy.55
  54.1 0.5 convolution_bitcast_fusion
  54.7 1.0 copy.49
  55.7 0.0 all-reduce.3.cloned.1.call-update
  55.8 1.3 dynamic-slice
  57.7 57.8 %all-reduce.3.cloned.1.call-done = f32[1,2,256,256]{3,1,0,2:T(2,128)} async-done(((f32[1,2,256,256]{3,1,0,2:T(2,128)}), f32[1,2,256,256]{3,1,0,2:T(2,128)}) %all-reduce.3.cloned.1.call-update) | async-done | bytes 524304
  115.5 0.9 constant_dynamic-slice_fusion
  116.4 12.0 %copy.50 = f32[1,2,16384]{1,0,2:T(1,128)} copy(f32[1,2,16384]{2,1,0:T(2,128)S(1)} %bitcast.70) | data formatting | bytes 262144 | tf_op jit(solution)/shard_map/reshape | solution.py:44
  128.4 0.5 broadcast.138
  128.9 74.5 %reduce.4 = f32[16384,2]{1,0:T(8,128)} reduce(f32[16384,1,2]{2,1,0:T(1,128)} %bitcast.68, f32[]{:T(128)} %broadcast.138), dimensions={1}, to_apply=%bitcast.61.reduce_sub_computation | reduce | bytes 262148
  203.4 7.6 %reshape.194 = f32[128,1,256]{2,1,0:T(1,128)S(1)} reshape(f32[16384,2]{1,0:T(8,128)} %reduce.4) | data formatting | bytes 262144
  211.0 25.3 %all_to_all.47 = f32[128,1,256]{2,1,0:T(1,128)S(1)} all-to-all(f32[128,1,256]{2,1,0:T(1,128)S(1)} %reshape.194), channel_id=1, replica_groups=mesh['grp'=4,'wide'=128] {'wide'}, dimensions={0} | all-to-all | bytes 262144 | tf_op jit(solution)/shard_map/all_to_all | solution.py:45
  236.3 1.0 reduce.5
  237.2 14.9 %reshape.195 = f32[16384,1,2]{2,1,0:T(1,128)} reshape(f32[128,256]{1,0:T(8,128)S(1)} %reduce.5) | data formatting | bytes 262144
  252.1 0.0 copy-start.1
  252.1 0.0 copy-start.2
  252.1 5.2 %copy.56 = f32[1,2,128,128]{3,2,1,0:T(8,128)S(1)} copy(f32[1,2,128,128]{1,3,2,0:T(8,128)} %bitcast.69) | data formatting | bytes 262144 | tf_op jit(solution)/shard_map/all_to_all | solution.py:45
  257.4 0.0 copy-done.1
  257.4 0.3 fusion.16
  257.7 0.0 copy-done.2
  257.7 0.3 fusion
  258.0 0.1 copy.52
  258.1 17.8 %all_to_all.48 = f32[128,1,128]{2,1,0:T(1,128)S(1)} all-to-all(f32[128,1,128]{2,1,0:T(1,128)S(1)} %copy.52), channel_id=1, replica_groups=mesh['grp'=4,'wide'=128] {'wide'}, dimensions={0} | all-to-all | bytes 131072 | tf_op jit(solution)/shard_map/all_to_all | solution.py:47
  275.9 0.5 broadcast.137
  276.4 0.8 reduce.3
  277.3 0.0 copy-done
  277.3 0.8 convolution_bitcast_fusion.1
  (4 shorter events, 0.1 us)
Async XLA Ops:
  6.5 270.7 %copy-start = (f32[1,256,128]{2,1,0:T(8,128)S(1)}, f32[1,256,128]{2,1,0:T(8,128)}, u32[]{:S(2)}) copy-start(f32[1,256,128]{2,1,0:T(8,128)} %param.7) | copy-start | bytes 393220
  6.5 109.0 %all-reduce.3.cloned.1.call-start = ((), (), s32[]{:S(2)}) async-start(), calls=%async_computation.3 | async-start | bytes 1048576
  252.1 5.3 %copy-start.1 = (f32[128,128]{1,0:T(8,128)S(1)}, f32[128,128]{1,0:T(8,128)}, u32[]{:S(2)}) copy-start(f32[128,128]{1,0:T(8,128)} %param.5) | copy-start | bytes 196612
  252.1 5.6 %copy-start.2 = (f32[128,128]{1,0:T(8,128)S(1)}, f32[128,128]{1,0:T(8,128)}, u32[]{:S(2)}) copy-start(f32[128,128]{1,0:T(8,128)} %param.6) | copy-start | bytes 196612
Sparse Core Ops, SparseCore 0:
  55.9 59.5 all-reduce.2
where the time goes:
time: 285 us
  other arithmetic  80.7 us (28%)
  blocking collectives  80.4 us (28%)
  waiting for transfers between devices  57.8 us (20%)
  local copies, waits for them, and re-layouts  46.5 us (16%)
  between operations  14.2 us (5%)
  matrix products  5.34 us (2%)
    unnamed x1, other arithmetic  74.5 us
    unnamed x2, waiting for transfers between devices  57.8 us
    all_to_all x1, blocking collectives, body(): lax.all_to_all(spectra, 'wide', split_axis=0, concat_axis=2, tiled=True)  37.3 us
    all_to_all x1, blocking collectives, body(): lax.all_to_all(flat, 'wide', split_axis=2, concat_axis=0, tiled=True)  25.3 us
    unnamed x11, local copies, waits for them, and re-layouts  25.2 us
    all_to_all x1, blocking collectives, body(): lax.all_to_all(degree_part, 'wide', split_axis=0, concat_axis=1, tiled=True)  17.8 us
    reshape x1, local copies, waits for them, and re-layouts, body(): flat = summed.reshape(own_harms, 2, radii // groups * radii)  12 us
  transfers between devices with their start and end apart: 1, of which 1 were waited for; matrix products, arithmetic and copies ran while one was open for 0% of the time, Pallas kernels for 0%

commit v1 on v0

v1 whole, which is shorter than its diff:
```python
import functools
import math

import jax
import jax.numpy as jnp
import ml_dtypes
import numpy as np
from jax import lax
from jax.experimental import pallas as pl
from jax.experimental.pallas import tpu as pltpu
from jax.sharding import PartitionSpec as P

HARMS = 128
LANES = 128


def table_rows(points, count):
    product = np.arange(count)[:, None] * np.arange(points)[None, :] % points
    phase = product.astype(np.float32) * np.float32(2.0 * math.pi / points)
    norm_scale = np.float32(1.0 / math.sqrt(points))
    both = np.concatenate([np.cos(phase) * norm_scale, -np.sin(phase) * norm_scale])
    return both.astype(ml_dtypes.bfloat16)


def spectra_kernel(img_ref, table_ref, out_ref, rows_ref):
    step = pl.program_id(0)
    count = pl.num_programs(0)
    harms = table_ref.shape[0] // 2
    both = lax.dot_general(
        table_ref[...], img_ref[0], (((1,), (1,)), ((), ())), preferred_element_type=jnp.float32
    )
    for lane in range(0, both.shape[1], LANES):
        cols = slice(lane, lane + LANES)
        rows_ref[lane // LANES, pl.ds(step, harms, stride=8), :] = both[:harms, cols]
        rows_ref[lane // LANES, pl.ds(step + 4, harms, stride=8), :] = both[harms:, cols]

    @pl.when(step == count - 1)
    def _():
        for half in range(rows_ref.shape[0]):
            out_ref[:, half * LANES:(half + 1) * LANES] = rows_ref[half].astype(jnp.bfloat16)


def spectra_call(images, table):
    count, radii, points = images.shape
    wide = table.shape[0]
    rows = wide * count
    return pl.pallas_call(
        spectra_kernel,
        grid=(count,),
        out_shape=jax.ShapeDtypeStruct((rows, radii), jnp.bfloat16),
        in_specs=[
            pl.BlockSpec((1, radii, points), lambda i: (i, 0, 0)),
            pl.BlockSpec((wide, points), lambda i: (0, 0), pipeline_mode=pl.Buffered(1)),
        ],
        out_specs=pl.BlockSpec((rows, radii), lambda i: (0, 0)),
        scratch_shapes=[pltpu.VMEM((radii // LANES, rows, LANES), jnp.float32)],
        name="spectra",
    )(images, table)


def gram_kernel(x_ref, own_ref, send_ref, gram_ref):
    core = lax.rem(lax.axis_index("grp"), 2)
    x = x_ref[...]
    rows, radii = x.shape
    wide = x.astype(jnp.float32).reshape(rows // 8, 8, radii)
    turned = pltpu.roll(wide, 4, 1)
    spot = lax.broadcasted_iota(jnp.int32, turned.shape, 1)
    turned = jnp.where(spot < 4, -turned, turned).reshape(rows, radii).astype(jnp.bfloat16)
    dims = (((0,), (0,)), ((), ()))
    gram_ref[:, :radii] = lax.dot_general(x, x, dims, preferred_element_type=jnp.float32)
    gram_ref[:, radii:] = lax.dot_general(x, turned, dims, preferred_element_type=jnp.float32)
    part = own_ref.shape[1]
    for top in range(2):
        mine = pl.multiple_of((2 * top + core) * part, 8)
        other = pl.multiple_of((2 * top + 1 - core) * part, 8)
        own_ref[top] = gram_ref[pl.ds(mine, part), :]
        send_ref[top] = gram_ref[pl.ds(other, part), :]


def gram_call(pooled):
    rows, radii = pooled.shape
    half = jax.ShapeDtypeStruct((2, radii // 4, 2 * radii), jnp.float32)
    return pl.pallas_call(
        gram_kernel,
        out_shape=(half, half),
        scratch_shapes=[pltpu.VMEM((radii, 2 * radii), jnp.float32)],
        name="gram",
    )(pooled)


def merge_kernel(scale, own_ref, got_ref, out_ref, rows_ref):
    radii = own_ref.shape[2] // 2
    part = own_ref.shape[1]
    for top in range(2):
        for half in range(2):
            for kind in range(2):
                cols = slice(kind * radii + half * LANES, kind * radii + (half + 1) * LANES)
                total = (own_ref[top, :, cols] + got_ref[top, :, cols]) * scale
                first = (top * 2 + half) * part * 2 + kind
                rows_ref[pl.ds(first, part, stride=2), :] = total
    out_ref[...] = rows_ref[...].astype(jnp.bfloat16)


def merge_call(own, got, total_img):
    rows = own.size // LANES
    return pl.pallas_call(
        functools.partial(merge_kernel, 1.0 / total_img),
        out_shape=jax.ShapeDtypeStruct((rows, LANES), jnp.bfloat16),
        scratch_shapes=[pltpu.VMEM((rows, LANES), jnp.float32)],
        name="merge",
    )(own, got)


def legendre_kernel(corr_ref, real_ref, imag_ref, out_ref, rows_ref):
    rows_ref[...] = corr_ref[...].astype(jnp.float32)
    harms = real_ref.shape[1]

    def summed(kind):
        low = rows_ref[pl.ds(kind, harms, stride=2), :]
        return low + rows_ref[pl.ds(2 * harms + kind, harms, stride=2), :]

    exact = functools.partial(
        jnp.dot, precision=lax.Precision.HIGHEST, preferred_element_type=jnp.float32
    )
    out_ref[...] = exact(real_ref[...], summed(0)) + exact(imag_ref[...], summed(1))


def legendre_call(corr, legendre_real, legendre_imag):
    degrees = legendre_real.shape[0]
    return pl.pallas_call(
        legendre_kernel,
        out_shape=jax.ShapeDtypeStruct((degrees, LANES), jnp.float32),
        scratch_shapes=[pltpu.VMEM(corr.shape, jnp.float32)],
        name="legendre",
    )(corr, legendre_real, legendre_imag)


def project_kernel(inv_ref, amp_ref, out_ref):
    part = inv_ref.shape[0] // 2
    exact = functools.partial(
        jnp.dot, precision=lax.Precision.HIGHEST, preferred_element_type=jnp.float32
    )
    low = exact(inv_ref[:part, :], amp_ref[0, :LANES, :])
    out_ref[0] = low + exact(inv_ref[part:, :], amp_ref[0, LANES:, :])


def project_call(inverted, amplitudes):
    return pl.pallas_call(
        project_kernel,
        out_shape=jax.ShapeDtypeStruct(
            (1, inverted.shape[0] // 2, amplitudes.shape[2]), jnp.float32
        ),
        name="project",
    )(inverted, amplitudes)


def body(images, legendre_real, legendre_imag, amplitudes):
    local_img, radii, points = images.shape
    groups = lax.axis_size("grp")
    owners = lax.axis_size("wide")
    total_img = local_img * groups * owners

    spectra = spectra_call(images, jnp.asarray(table_rows(points, HARMS)))
    spectra = spectra.reshape(HARMS, 2 * local_img, radii)
    pooled = lax.all_to_all(spectra, "wide", split_axis=0, concat_axis=0, tiled=True)

    own, send = gram_call(pooled.reshape(HARMS * 2 * local_img, radii))
    swap = [(g * owners + w, (g ^ 1) * owners + w) for g in range(groups) for w in range(owners)]
    got = lax.ppermute(send, ("grp", "wide"), swap)
    corr = merge_call(own, got, total_img)

    columns = [
        [(2 * top + core) * owners + w for top in range(2) for w in range(owners)]
        for core in range(2)
    ]
    every_harm = lax.all_to_all(
        corr.reshape(2 * owners, 2, LANES), ("grp", "wide"), split_axis=0, concat_axis=0,
        axis_index_groups=columns, tiled=True,
    )
    degree_part = legendre_call(
        every_harm.reshape(4 * owners, LANES), legendre_real, legendre_imag
    )
    mine = lax.all_to_all(
        degree_part.reshape(owners, 1, LANES), "wide", split_axis=0, concat_axis=0, tiled=True
    )
    return project_call(mine.reshape(owners, LANES), amplitudes)


def solution(mesh):
    return jax.shard_map(
        body,
        mesh=mesh,
        in_specs=(P(("grp", "wide"), None, None), P(), P(), P("wide", None, None)),
        out_specs=P("wide", "grp", None),
        check_vma=False,
    )
```

time: 285 us -> 102 us (0.36)
  other arithmetic: 80.7 us -> 0 us
  waiting for transfers between devices: 57.8 us -> 1.71 us
  local copies, waits for them, and re-layouts: 46.5 us -> 0.69 us
  between operations: 14.2 us -> 0.01 us
  Pallas kernels: 0 us -> 12.9 us
  matrix products: 5.34 us -> 0 us
  blocking collectives: 80.4 us -> 84.4 us
    unnamed x1 -> x0, other arithmetic: 74.5 us -> none
    unnamed x2 -> x0, waiting for transfers between devices: 57.8 us -> none
    unnamed x11 -> x2, local copies, waits for them, and re-layouts: 25.2 us -> 0.69 us
    pallas_call x0 -> x5, Pallas kernels: none -> 12.9 us  [the longest x1 5.18 us: spectra_call(): pl.pallas_call(spectra_kernel, grid=(count,), out_shape=jax.ShapeDtypeStr...]
    reshape x2 -> x0, local copies, waits for them, and re-layouts: 12.4 us -> none  [the longest x1 12 us: body(): flat = summed.reshape(own_harms, 2, radii // groups * radii)]
    all_to_all x3 -> x0, local copies, waits for them, and re-layouts: 5.85 us -> none  [the longest x1 5.25 us: body(): lax.all_to_all(flat, 'wide', split_axis=2, concat_axis=0, tiled=True)]
    dot_general x5 -> x0, matrix products: 5.34 us -> none  [the longest x1 3.47 us: body(): lax.dot_general(table_rows, flat_images, (((1,), (1,)), ((), ())), prefer...]
    another operation x3 -> x0, other arithmetic: 4.46 us -> none
where the time goes in v1:
time: 102 us
  blocking collectives  84.4 us (83%)
  Pallas kernels  12.9 us (13%)
  starting transfers between devices  1.91 us (2%)
  waiting for transfers between devices  1.71 us (2%)
    all_to_all x1, blocking collectives, body(): lax.all_to_all(spectra, 'wide', split_axis=0, concat_axis=0, tiled=True)  37.6 us
    all_to_all x1, blocking collectives, body(): lax.all_to_all(corr.reshape(2 * owners, 2, LANES), ('grp', 'wide'), split...  27 us
    all_to_all x1, blocking collectives, body(): lax.all_to_all(degree_part.reshape(owners, 1, LANES), 'wide', split_axis=...  19.8 us
    pallas_call x1, Pallas kernels, spectra_call(): pl.pallas_call(spectra_kernel, grid=(count,), out_shape=jax.ShapeDtypeStr...  5.18 us
    pallas_call x1, Pallas kernels, gram_call(): pl.pallas_call(gram_kernel, out_shape=(half, half), scratch_shapes=[pltpu...  2.36 us
  transfers between devices with their start and end apart: 1, of which 1 were waited for; matrix products, arithmetic and copies ran while one was open for 0% of the time, Pallas kernels for 0%

profile of v1, /device:TPU:8, one launch (start us, length us, event | category | flops | bytes accessed | tf_op | source)
XLA Modules:
  0.0 101.6 jit_solution(3735134791527596058)
XLA Ops:
  0.0 5.2 %spectra.1 = bf16[1024,256]{1,0:T(8,128)(2,1)} custom-call(bf16[4,256,2048]{2,1,0:T(8,128)(2,1)} %img_ref.1, bf16[256,2048]{1,0:T(8,128)(2,1)} %constant.2.clone.table_ref), custom_call_target="tpu_custom_call" | custom-call | tf_op jit(solution)/shard_map/spectra/pallas_call | solution.py:47
  5.2 37.6 %all_to_all.15 = bf16[128,8,256]{2,1,0:T(8,128)(2,1)} all-to-all(bf16[128,8,256]{2,1,0:T(8,128)(2,1)} %bitcast.9), channel_id=1, replica_groups=mesh['grp'=4,'wide'=128] {'wide'}, dimensions={0} | all-to-all | bytes 1048576 | tf_op jit(solution)/shard_map/all_to_all | solution.py:165
  42.8 2.4 %gram.1 = (f32[2,64,512]{2,1,0:T(8,128)}, f32[2,64,512]{2,1,0:T(8,128)}) custom-call(bf16[1024,256]{1,0:T(8,128)(2,1)} %bitcast.8), custom_call_target="tpu_custom_call" | custom-call | tf_op jit(solution)/shard_map/gram/pallas_call | solution.py:83
  45.1 1.9 %collective-permute-start = (f32[2,64,512]{2,1,0:T(8,128)}, f32[2,64,512]{2,1,0:T(8,128)S(1)}, u32[]{:S(2)}, u32[]{:S(2)}) collective-permute-start(f32[2,64,512]{2,1,0:T(8,128)} %get-tuple-element.8), channel_id=1, source_target_pairs={{0,128},{1,129},{2,130},{3,131},{4,132},{5,133},{6,134},{7,135},{8... | collective-permute-start | bytes 786440 | tf_op jit(solution)/shard_map/ppermute | solution.py:169
  47.0 1.7 %collective-permute-done.got_ref = f32[2,64,512]{2,1,0:T(8,128)S(1)} collective-permute-done((f32[2,64,512]{2,1,0:T(8,128)}, f32[2,64,512]{2,1,0:T(8,128)S(1)}, u32[]{:S(2)}, u32[]{:S(2)}) %collective-permute-start) | collective-permute-done | bytes 262176 | tf_op jit(solution)/shard_map/ppermute | solution.py:169
  48.8 0.0 copy-start
  48.8 0.7 copy-done
  49.4 1.7 %merge.1 = bf16[512,128]{1,0:T(8,128)(2,1)} custom-call(f32[2,64,512]{2,1,0:T(8,128)} %get-tuple-element.7.own_ref, f32[2,64,512]{2,1,0:T(8,128)} %copy-done), custom_call_target="tpu_custom_call" | custom-call | tf_op jit(solution)/shard_map/merge/pallas_call | solution.py:106
  51.2 27.0 %all_to_all.16 = bf16[256,2,128]{2,1,0:T(2,128)(2,1)} all-to-all(bf16[256,2,128]{2,1,0:T(2,128)(2,1)} %bitcast.10), channel_id=1, replica_groups={{0,1,2,3,4,5,6,7,8,9,10,11,12,13,14,15,16,17,18,19,20,21,22,23,24,25,26..., dimensions={0} | all-to-all | bytes 262144 | tf_op jit(solution)/shard_map/all_to_all | solution.py:176
  78.2 1.9 %legendre.1 = f32[128,128]{1,0:T(8,128)} custom-call(bf16[512,128]{1,0:T(8,128)(2,1)} %bitcast.11, f32[128,128]{1,0:T(8,128)} %real_ref.1, f32[128,128]{1,0:T(8,128)} %imag_ref.1), custom_call_target="tpu_custom_call" | custom-call | tf_op jit(solution)/shard_map/legendre/pallas_call | solution.py:130
  80.0 19.8 %all_to_all.17 = f32[128,1,128]{2,1,0:T(1,128)} all-to-all(f32[128,1,128]{2,1,0:T(1,128)} %bitcast.12), channel_id=1, replica_groups=mesh['grp'=4,'wide'=128] {'wide'}, dimensions={0} | all-to-all | bytes 131072 | tf_op jit(solution)/shard_map/all_to_all | solution.py:183
  99.8 1.8 %project.1 = f32[1,64,128]{2,1,0:T(8,128)} custom-call(f32[128,128]{1,0:T(8,128)} %bitcast.13, f32[1,256,128]{2,1,0:T(8,128)} %amp_ref.1), custom_call_target="tpu_custom_call" | custom-call | tf_op jit(solution)/shard_map/project/pallas_call | solution.py:148
Async XLA Ops:
  45.1 3.6 %collective-permute-start = (f32[2,64,512]{2,1,0:T(8,128)}, f32[2,64,512]{2,1,0:T(8,128)S(1)}, u32[]{:S(2)}, u32[]{:S(2)}) collective-permute-start(f32[2,64,512]{2,1,0:T(8,128)} %get-tuple-element.8), channel_id=1, source_target_pairs={{0,128},{1,129},{2,130},{3,131},{4,132},{5,133},{6,134},{7,135},{8... | collective-permute-start | bytes 786440 | tf_op jit(solution)/shard_map/ppermute | solution.py:169
  48.8 0.7 copy-start

commit v2 on v1

--- a/solution.py
+++ b/solution.py
@@ -22,22 +22,34 @@
     return both.astype(ml_dtypes.bfloat16)
 
 
-def spectra_kernel(img_ref, table_ref, out_ref, rows_ref):
-    step = pl.program_id(0)
-    count = pl.num_programs(0)
+def spectra_kernel(img_hbm, table_hbm, out_ref, img_ref, table_ref, rows_ref, img_sem, table_sem):
+    count = img_ref.shape[0]
     harms = table_ref.shape[0] // 2
-    both = lax.dot_general(
-        table_ref[...], img_ref[0], (((1,), (1,)), ((), ())), preferred_element_type=jnp.float32
-    )
-    for lane in range(0, both.shape[1], LANES):
-        cols = slice(lane, lane + LANES)
-        rows_ref[lane // LANES, pl.ds(step, harms, stride=8), :] = both[:harms, cols]
-        rows_ref[lane // LANES, pl.ds(step + 4, harms, stride=8), :] = both[harms:, cols]
-
-    @pl.when(step == count - 1)
-    def _():
-        for half in range(rows_ref.shape[0]):
-            out_ref[:, half * LANES:(half + 1) * LANES] = rows_ref[half].astype(jnp.bfloat16)
+    table_copy = pltpu.make_async_copy(table_hbm, table_ref, table_sem)
+    table_copy.start()
+
+    def image_copy(i):
+        return pltpu.make_async_copy(img_hbm.at[i], img_ref.at[i], img_sem.at[i])
+
+    @pl.loop(0, count)
+    def _(i):
+        image_copy(i).start()
+
+    table_copy.wait()
+
+    @pl.loop(0, count)
+    def _(i):
+        image_copy(i).wait()
+        both = lax.dot_general(
+            table_ref[...], img_ref[i], (((1,), (1,)), ((), ())), preferred_element_type=jnp.float32
+        )
+        for half in range(both.shape[1] // LANES):
+            cols = slice(half * LANES, (half + 1) * LANES)
+            rows_ref[half, pl.ds(i, harms, stride=8), :] = both[:harms, cols]
+            rows_ref[half, pl.ds(i + 4, harms, stride=8), :] = both[harms:, cols]
+
+    for half in range(rows_ref.shape[0]):
+        out_ref[:, half * LANES:(half + 1) * LANES] = rows_ref[half].astype(jnp.bfloat16)
 
 
 def spectra_call(images, table):
@@ -46,16 +58,21 @@
     rows = wide * count
     return pl.pallas_call(
         spectra_kernel,
-        grid=(count,),
         out_shape=jax.ShapeDtypeStruct((rows, radii), jnp.bfloat16),
-        in_specs=[
-            pl.BlockSpec((1, radii, points), lambda i: (i, 0, 0)),
-            pl.BlockSpec((wide, points), lambda i: (0, 0), pipeline_mode=pl.Buffered(1)),
+        in_specs=[pl.BlockSpec(memory_space=pltpu.HBM)] * 2,
+        scratch_shapes=[
+            pltpu.VMEM(images.shape, jnp.bfloat16),
+            pltpu.VMEM(table.shape, jnp.bfloat16),
+            pltpu.VMEM((radii // LANES, rows, LANES), jnp.float32),
+            pltpu.SemaphoreType.DMA((count,)),
+            pltpu.SemaphoreType.DMA(()),
         ],
-        out_specs=pl.BlockSpec((rows, radii), lambda i: (0, 0)),
-        scratch_shapes=[pltpu.VMEM((radii // LANES, rows, LANES), jnp.float32)],
+        compiler_params=pltpu.CompilerParams(vmem_limit_bytes=16 << 20),
         name="spectra",
-    )(images, table)
+    )(
+        pltpu.with_memory_space_constraint(images, pltpu.HBM),
+        pltpu.with_memory_space_constraint(table, pltpu.HBM),
+    )
 
 
 def gram_kernel(x_ref, own_ref, send_ref, gram_ref):
@@ -84,6 +101,7 @@
         gram_kernel,
         out_shape=(half, half),
         scratch_shapes=[pltpu.VMEM((radii, 2 * radii), jnp.float32)],
+        compiler_params=pltpu.CompilerParams(vmem_limit_bytes=8 << 20),
         name="gram",
     )(pooled)
 
@@ -107,6 +125,7 @@
         functools.partial(merge_kernel, 1.0 / total_img),
         out_shape=jax.ShapeDtypeStruct((rows, LANES), jnp.bfloat16),
         scratch_shapes=[pltpu.VMEM((rows, LANES), jnp.float32)],
+        compiler_params=pltpu.CompilerParams(vmem_limit_bytes=8 << 20),
         name="merge",
     )(own, got)
 
@@ -131,6 +150,7 @@
         legendre_kernel,
         out_shape=jax.ShapeDtypeStruct((degrees, LANES), jnp.float32),
         scratch_shapes=[pltpu.VMEM(corr.shape, jnp.float32)],
+        compiler_params=pltpu.CompilerParams(vmem_limit_bytes=8 << 20),
         name="legendre",
     )(corr, legendre_real, legendre_imag)
 
@@ -150,6 +170,7 @@
         out_shape=jax.ShapeDtypeStruct(
             (1, inverted.shape[0] // 2, amplitudes.shape[2]), jnp.float32
         ),
+        compiler_params=pltpu.CompilerParams(vmem_limit_bytes=8 << 20),
         name="project",
     )(inverted, amplitudes)
 

time: 102 us -> 90.5 us (0.89)
  the two profiles are of different devices: /device:TPU:8 before, /device:TPU:2 now
where the time goes in v2:
time: 90.5 us; the launch traced here: 90.3 us
  blocking collectives  81.5 us (90%)
  Pallas kernels  5.34 us (6%)
  starting transfers between devices  1.92 us (2%)
  waiting for transfers between devices  1.5 us (2%)
    all_to_all x1, blocking collectives, body(): lax.all_to_all(spectra, 'wide', split_axis=0, concat_axis=0, tiled=True)  35.2 us
    all_to_all x1, blocking collectives, body(): lax.all_to_all(corr.reshape(2 * owners, 2, LANES), ('grp', 'wide'), split...  28.2 us
    all_to_all x1, blocking collectives, body(): lax.all_to_all(degree_part.reshape(owners, 1, LANES), 'wide', split_axis=...  18.1 us
    pallas_call x1, Pallas kernels, spectra_call(): pl.pallas_call(spectra_kernel, out_shape=jax.ShapeDtypeStruct((rows, radi...  3.64 us
    ppermute x1, starting transfers between devices, body(): got = lax.ppermute(send, ('grp', 'wide'), swap)  1.92 us
  transfers between devices with their start and end apart: 1, of which 1 were waited for; matrix products, arithmetic and copies ran while one was open for 0% of the time, Pallas kernels for 0%

profile of v2, /device:TPU:2, one launch (start us, length us, event | category | flops | bytes accessed | tf_op | source)
XLA Modules:
  0.0 90.3 jit_solution(851035710714840270)
XLA Ops:
  0.0 0.0 copy-start.2
  0.0 0.0 copy-start.1
  0.0 0.0 copy-start
  0.0 3.6 %spectra.1 = bf16[1024,256]{1,0:T(8,128)(2,1)S(1)} custom-call(bf16[4,256,2048]{2,1,0:T(8,128)(2,1)} %img_hbm.1, bf16[256,2048]{1,0:T(8,128)(2,1)} %constant.2.clone.table_hbm), custom_call_target="tpu_custom_call" | custom-call | tf_op jit(solution)/shard_map/spectra/pallas_call | solution.py:59
  3.7 35.2 %all_to_all.15 = bf16[128,8,256]{2,1,0:T(8,128)(2,1)S(1)} all-to-all(bf16[128,8,256]{2,1,0:T(8,128)(2,1)S(1)} %bitcast.9), channel_id=1, replica_groups=mesh['grp'=4,'wide'=128] {'wide'}, dimensions={0} | all-to-all | bytes 1048576 | tf_op jit(solution)/shard_map/all_to_all | solution.py:186
  38.9 0.5 gram.1
  39.4 1.9 %collective-permute-start = (f32[2,64,512]{2,1,0:T(8,128)S(1)}, f32[2,64,512]{2,1,0:T(8,128)S(1)}, u32[]{:S(2)}, u32[]{:S(2)}) collective-permute-start(f32[2,64,512]{2,1,0:T(8,128)S(1)} %get-tuple-element.8), channel_id=1, source_target_pairs={{0,128},{1,129},{2,130},{3,131},{4,132},{5,133},{6,134},{7,135},{8... | collective-permute-start | bytes 786440 | tf_op jit(solution)/shard_map/ppermute | solution.py:190
  41.3 1.5 %collective-permute-done.got_ref = f32[2,64,512]{2,1,0:T(8,128)S(1)} collective-permute-done((f32[2,64,512]{2,1,0:T(8,128)S(1)}, f32[2,64,512]{2,1,0:T(8,128)S(1)}, u32[]{:S(2)}, u32[]{:S(2)}) %collective-permute-start) | collective-permute-done | bytes 262176 | tf_op jit(solution)/shard_map/ppermute | solution.py:190
  42.9 28.2 %all_to_all.16 = bf16[256,2,128]{2,1,0:T(2,128)(2,1)S(1)} all-to-all(bf16[256,2,128]{2,1,0:T(2,128)(2,1)S(1)} %bitcast.10), channel_id=1, replica_groups={{0,1,2,3,4,5,6,7,8,9,10,11,12,13,14,15,16,17,18,19,20,21,22,23,24,25,26..., dimensions={0} | all-to-all | bytes 262144 | tf_op jit(solution)/shard_map/all_to_all | solution.py:197
  71.1 0.0 copy-done.2
  71.1 0.0 copy-done.1
  71.1 0.3 legendre.1
  71.4 18.1 %all_to_all.17 = f32[128,1,128]{2,1,0:T(1,128)S(1)} all-to-all(f32[128,1,128]{2,1,0:T(1,128)S(1)} %bitcast.12), channel_id=1, replica_groups=mesh['grp'=4,'wide'=128] {'wide'}, dimensions={0} | all-to-all | bytes 131072 | tf_op jit(solution)/shard_map/all_to_all | solution.py:204
  89.4 0.0 copy-done
  89.4 0.9 project.1
  (1 shorter events, 0.0 us)
Async XLA Ops:
  0.0 71.1 %copy-start.2 = (f32[128,128]{1,0:T(8,128)S(1)}, f32[128,128]{1,0:T(8,128)}, u32[]{:S(2)}) copy-start(f32[128,128]{1,0:T(8,128)} %imag_ref.1) | copy-start | bytes 196612
  0.0 71.1 %copy-start.1 = (f32[128,128]{1,0:T(8,128)S(1)}, f32[128,128]{1,0:T(8,128)}, u32[]{:S(2)}) copy-start(f32[128,128]{1,0:T(8,128)} %real_ref.1) | copy-start | bytes 196612
  0.0 89.4 %copy-start = (f32[1,256,128]{2,1,0:T(8,128)S(1)}, f32[1,256,128]{2,1,0:T(8,128)}, u32[]{:S(2)}) copy-start(f32[1,256,128]{2,1,0:T(8,128)} %amp_ref.1) | copy-start | bytes 393220
  39.4 3.4 %collective-permute-start = (f32[2,64,512]{2,1,0:T(8,128)S(1)}, f32[2,64,512]{2,1,0:T(8,128)S(1)}, u32[]{:S(2)}, u32[]{:S(2)}) collective-permute-start(f32[2,64,512]{2,1,0:T(8,128)S(1)} %get-tuple-element.8), channel_id=1, source_target_pairs={{0,128},{1,129},{2,130},{3,131},{4,132},{5,133},{6,134},{7,135},{8... | collective-permute-start | bytes 786440 | tf_op jit(solution)/shard_map/ppermute | solution.py:190

commit v3 on v2

--- a/solution.py
+++ b/solution.py
@@ -22,6 +22,13 @@
     return both.astype(ml_dtypes.bfloat16)
 
 
+def skewed_order():
+    return [
+        ((z + x + y) % 4 * 4 + (x + y) % 4) * 8 + y
+        for z in range(4) for x in range(4) for y in range(8)
+    ]
+
+
 def spectra_kernel(img_hbm, table_hbm, out_ref, img_ref, table_ref, rows_ref, img_sem, table_sem):
     count = img_ref.shape[0]
     harms = table_ref.shape[0] // 2
@@ -37,14 +44,21 @@
 
     table_copy.wait()
 
-    @pl.loop(0, count)
-    def _(i):
-        image_copy(i).wait()
+    @pl.loop(0, count // 2)
+    def _(pair):
+        image_copy(2 * pair).wait()
+        image_copy(2 * pair + 1).wait()
         both = lax.dot_general(
-            table_ref[...], img_ref[i], (((1,), (1,)), ((), ())), preferred_element_type=jnp.float32
+            table_ref[...],
+            img_ref[pl.ds(2 * pair, 2)].reshape(-1, img_ref.shape[2]),
+            (((1,), (1,)), ((), ())),
+            preferred_element_type=jnp.float32,
         )
-        for half in range(both.shape[1] // LANES):
-            cols = slice(half * LANES, (half + 1) * LANES)
+        halves = rows_ref.shape[0]
+        for part in range(2 * halves):
+            i = 2 * pair + part // halves
+            half = part % halves
+            cols = slice(part * LANES, (part + 1) * LANES)
             rows_ref[half, pl.ds(i, harms, stride=8), :] = both[:harms, cols]
             rows_ref[half, pl.ds(i + 4, harms, stride=8), :] = both[harms:, cols]
 
@@ -141,7 +155,15 @@
     exact = functools.partial(
         jnp.dot, precision=lax.Precision.HIGHEST, preferred_element_type=jnp.float32
     )
-    out_ref[...] = exact(real_ref[...], summed(0)) + exact(imag_ref[...], summed(1))
+    result = exact(real_ref[...], summed(0)) + exact(imag_ref[...], summed(1))
+    tiles = result.reshape(result.shape[0] // 8, 8, LANES)
+    spot = lax.broadcasted_iota(jnp.int32, (8, LANES), 0) % 4
+    for z in range(4):
+        for x in range(4):
+            rows = tiles[z * 4 + x]
+            for y in range(4):
+                rows = jnp.where(spot == y, tiles[(z + x + y) % 4 * 4 + (x + y) % 4], rows)
+            out_ref[(z * 4 + x) * 8:(z * 4 + x + 1) * 8, :] = rows
 
 
 def legendre_call(corr, legendre_real, legendre_imag):
@@ -183,7 +205,11 @@
 
     spectra = spectra_call(images, jnp.asarray(table_rows(points, HARMS)))
     spectra = spectra.reshape(HARMS, 2 * local_img, radii)
-    pooled = lax.all_to_all(spectra, "wide", split_axis=0, concat_axis=0, tiled=True)
+    order = skewed_order()
+    rings = [[g * owners + w for w in order] for g in range(groups)]
+    pooled = lax.all_to_all(
+        spectra, ("grp", "wide"), split_axis=0, concat_axis=0, axis_index_groups=rings, tiled=True
+    )
 
     own, send = gram_call(pooled.reshape(HARMS * 2 * local_img, radii))
     swap = [(g * owners + w, (g ^ 1) * owners + w) for g in range(groups) for w in range(owners)]
@@ -191,7 +217,7 @@
     corr = merge_call(own, got, total_img)
 
     columns = [
-        [(2 * top + core) * owners + w for top in range(2) for w in range(owners)]
+        [(2 * top + core) * owners + w for top in range(2) for w in order]
         for core in range(2)
     ]
     every_harm = lax.all_to_all(
@@ -202,7 +228,8 @@
         every_harm.reshape(4 * owners, LANES), legendre_real, legendre_imag
     )
     mine = lax.all_to_all(
-        degree_part.reshape(owners, 1, LANES), "wide", split_axis=0, concat_axis=0, tiled=True
+        degree_part.reshape(owners, 1, LANES), ("grp", "wide"), split_axis=0, concat_axis=0,
+        axis_index_groups=rings, tiled=True,
     )
     return project_call(mine.reshape(owners, LANES), amplitudes)
 

time: 90.5 us -> 89.6 us (0.990)
  the two profiles are of different devices: /device:TPU:2 before, /device:TPU:8 now
where the time goes in v3:
time: 89.6 us; the launch traced here: 89.4 us
  blocking collectives  80.6 us (90%)
  Pallas kernels  5.27 us (6%)
  starting transfers between devices  1.92 us (2%)
  waiting for transfers between devices  1.5 us (2%)
    all_to_all x1, blocking collectives, body(): lax.all_to_all(spectra, ('grp', 'wide'), split_axis=0, concat_axis=0, axi...  36.6 us
    all_to_all x1, blocking collectives, body(): lax.all_to_all(corr.reshape(2 * owners, 2, LANES), ('grp', 'wide'), split...  27.4 us
    all_to_all x1, blocking collectives, body(): lax.all_to_all(degree_part.reshape(owners, 1, LANES), ('grp', 'wide'), sp...  16.6 us
    pallas_call x1, Pallas kernels, spectra_call(): pl.pallas_call(spectra_kernel, out_shape=jax.ShapeDtypeStruct((rows, radi...  3.56 us
    ppermute x1, starting transfers between devices, body(): got = lax.ppermute(send, ('grp', 'wide'), swap)  1.92 us
  transfers between devices with their start and end apart: 1, of which 1 were waited for; matrix products, arithmetic and copies ran while one was open for 0% of the time, Pallas kernels for 0%

profile of v3, /device:TPU:8, one launch (start us, length us, event | category | flops | bytes accessed | tf_op | source)
XLA Modules:
  0.0 89.4 jit_solution(5621620124217978436)
XLA Ops:
  0.0 0.0 copy-start.2
  0.0 0.0 copy-start.1
  0.0 0.0 copy-start
  0.0 3.6 %spectra.1 = bf16[1024,256]{1,0:T(8,128)(2,1)S(1)} custom-call(bf16[4,256,2048]{2,1,0:T(8,128)(2,1)} %img_hbm.1, bf16[256,2048]{1,0:T(8,128)(2,1)} %constant.2.clone.table_hbm), custom_call_target="tpu_custom_call" | custom-call | tf_op jit(solution)/shard_map/spectra/pallas_call | solution.py:73
  3.6 36.6 %all_to_all.15 = bf16[128,8,256]{2,1,0:T(8,128)(2,1)S(1)} all-to-all(bf16[128,8,256]{2,1,0:T(8,128)(2,1)S(1)} %bitcast.9), channel_id=1, replica_groups={{0,41,82,123,4,45,86,127,40,81,122,3,44,85,126,7,80,121,2,43,84,125,6,4..., dimensions={0} | all-to-all | bytes 1048576 | tf_op jit(solution)/shard_map/all_to_all | solution.py:210
  40.1 0.5 gram.1
  40.7 1.9 %collective-permute-start = (f32[2,64,512]{2,1,0:T(8,128)S(1)}, f32[2,64,512]{2,1,0:T(8,128)S(1)}, u32[]{:S(2)}, u32[]{:S(2)}) collective-permute-start(f32[2,64,512]{2,1,0:T(8,128)S(1)} %get-tuple-element.8), channel_id=1, source_target_pairs={{0,128},{1,129},{2,130},{3,131},{4,132},{5,133},{6,134},{7,135},{8... | collective-permute-start | bytes 786440 | tf_op jit(solution)/shard_map/ppermute | solution.py:216
  42.6 1.5 %collective-permute-done.got_ref = f32[2,64,512]{2,1,0:T(8,128)S(1)} collective-permute-done((f32[2,64,512]{2,1,0:T(8,128)S(1)}, f32[2,64,512]{2,1,0:T(8,128)S(1)}, u32[]{:S(2)}, u32[]{:S(2)}) %collective-permute-start) | collective-permute-done | bytes 262176 | tf_op jit(solution)/shard_map/ppermute | solution.py:216
  44.1 27.4 %all_to_all.16 = bf16[256,2,128]{2,1,0:T(2,128)(2,1)S(1)} all-to-all(bf16[256,2,128]{2,1,0:T(2,128)(2,1)S(1)} %bitcast.10), channel_id=1, replica_groups={{0,41,82,123,4,45,86,127,40,81,122,3,44,85,126,7,80,121,2,43,84,125,6,4..., dimensions={0} | all-to-all | bytes 262144 | tf_op jit(solution)/shard_map/all_to_all | solution.py:223
  71.6 0.0 copy-done.2
  71.6 0.0 copy-done.1
  71.6 0.3 legendre.1
  71.9 16.6 %all_to_all.17 = f32[128,1,128]{2,1,0:T(1,128)S(1)} all-to-all(f32[128,1,128]{2,1,0:T(1,128)S(1)} %bitcast.12), channel_id=1, replica_groups={{0,41,82,123,4,45,86,127,40,81,122,3,44,85,126,7,80,121,2,43,84,125,6,4..., dimensions={0} | all-to-all | bytes 131072 | tf_op jit(solution)/shard_map/all_to_all | solution.py:230
  88.5 0.0 copy-done
  88.5 0.9 project.1
  (1 shorter events, 0.0 us)
Async XLA Ops:
  0.0 71.6 %copy-start.2 = (f32[128,128]{1,0:T(8,128)S(1)}, f32[128,128]{1,0:T(8,128)}, u32[]{:S(2)}) copy-start(f32[128,128]{1,0:T(8,128)} %imag_ref.1) | copy-start | bytes 196612
  0.0 71.6 %copy-start.1 = (f32[128,128]{1,0:T(8,128)S(1)}, f32[128,128]{1,0:T(8,128)}, u32[]{:S(2)}) copy-start(f32[128,128]{1,0:T(8,128)} %real_ref.1) | copy-start | bytes 196612
  0.0 88.5 %copy-start = (f32[1,256,128]{2,1,0:T(8,128)S(1)}, f32[1,256,128]{2,1,0:T(8,128)}, u32[]{:S(2)}) copy-start(f32[1,256,128]{2,1,0:T(8,128)} %amp_ref.1) | copy-start | bytes 393220
  40.7 3.4 %collective-permute-start = (f32[2,64,512]{2,1,0:T(8,128)S(1)}, f32[2,64,512]{2,1,0:T(8,128)S(1)}, u32[]{:S(2)}, u32[]{:S(2)}) collective-permute-start(f32[2,64,512]{2,1,0:T(8,128)S(1)} %get-tuple-element.8), channel_id=1, source_target_pairs={{0,128},{1,129},{2,130},{3,131},{4,132},{5,133},{6,134},{7,135},{8... | collective-permute-start | bytes 786440 | tf_op jit(solution)/shard_map/ppermute | solution.py:216

commit v4 on v3

--- a/solution.py
+++ b/solution.py
@@ -18,8 +18,9 @@
     product = np.arange(count)[:, None] * np.arange(points)[None, :] % points
     phase = product.astype(np.float32) * np.float32(2.0 * math.pi / points)
     norm_scale = np.float32(1.0 / math.sqrt(points))
-    both = np.concatenate([np.cos(phase) * norm_scale, -np.sin(phase) * norm_scale])
-    return both.astype(ml_dtypes.bfloat16)
+    real, imag = np.cos(phase) * norm_scale, -np.sin(phase) * norm_scale
+    both = [np.concatenate([real, imag]), np.concatenate([real[::-1], imag[::-1]])]
+    return np.stack(both).astype(ml_dtypes.bfloat16)
 
 
 def skewed_order():
@@ -32,7 +33,8 @@
 def spectra_kernel(img_hbm, table_hbm, out_ref, img_ref, table_ref, rows_ref, img_sem, table_sem):
     count = img_ref.shape[0]
     harms = table_ref.shape[0] // 2
-    table_copy = pltpu.make_async_copy(table_hbm, table_ref, table_sem)
+    core = lax.rem(lax.axis_index("grp"), 2)
+    table_copy = pltpu.make_async_copy(table_hbm.at[core], table_ref, table_sem)
     table_copy.start()
 
     def image_copy(i):
@@ -68,7 +70,7 @@
 
 def spectra_call(images, table):
     count, radii, points = images.shape
-    wide = table.shape[0]
+    wide = table.shape[1]
     rows = wide * count
     return pl.pallas_call(
         spectra_kernel,
@@ -76,7 +78,7 @@
         in_specs=[pl.BlockSpec(memory_space=pltpu.HBM)] * 2,
         scratch_shapes=[
             pltpu.VMEM(images.shape, jnp.bfloat16),
-            pltpu.VMEM(table.shape, jnp.bfloat16),
+            pltpu.VMEM(table.shape[1:], jnp.bfloat16),
             pltpu.VMEM((radii // LANES, rows, LANES), jnp.float32),
             pltpu.SemaphoreType.DMA((count,)),
             pltpu.SemaphoreType.DMA(()),
@@ -207,8 +209,9 @@
     spectra = spectra.reshape(HARMS, 2 * local_img, radii)
     order = skewed_order()
     rings = [[g * owners + w for w in order] for g in range(groups)]
+    both_ways = [ring[::-1] if g % 2 else ring for g, ring in enumerate(rings)]
     pooled = lax.all_to_all(
-        spectra, ("grp", "wide"), split_axis=0, concat_axis=0, axis_index_groups=rings, tiled=True
+        spectra, ("grp", "wide"), split_axis=0, concat_axis=0, axis_index_groups=both_ways, tiled=True
     )
 
     own, send = gram_call(pooled.reshape(HARMS * 2 * local_img, radii))

time: 89.6 us -> 88.2 us (0.984)
  blocking collectives: 80.6 us -> 79.2 us
    all_to_all x1, blocking collectives: 36.6 us -> 32.7 us  [body(): lax.all_to_all(spectra, ('grp', 'wide'), split_axis=0, concat_axis=0, axi...]
    all_to_all x1, blocking collectives: 27.4 us -> 29.9 us  [body(): lax.all_to_all(corr.reshape(2 * owners, 2, LANES), ('grp', 'wide'), split...]
where the time goes in v4:
time: 88.2 us; the launch traced here: 88 us
  blocking collectives  79.2 us (90%)
  Pallas kernels  5.28 us (6%)
  starting transfers between devices  1.92 us (2%)
  waiting for transfers between devices  1.5 us (2%)
    all_to_all x1, blocking collectives, body(): lax.all_to_all(spectra, ('grp', 'wide'), split_axis=0, concat_axis=0, axi...  32.7 us
    all_to_all x1, blocking collectives, body(): lax.all_to_all(corr.reshape(2 * owners, 2, LANES), ('grp', 'wide'), split...  29.9 us
    all_to_all x1, blocking collectives, body(): lax.all_to_all(degree_part.reshape(owners, 1, LANES), ('grp', 'wide'), sp...  16.6 us
    pallas_call x1, Pallas kernels, spectra_call(): pl.pallas_call(spectra_kernel, out_shape=jax.ShapeDtypeStruct((rows, radi...  3.57 us
    ppermute x1, starting transfers between devices, body(): got = lax.ppermute(send, ('grp', 'wide'), swap)  1.92 us
  transfers between devices with their start and end apart: 1, of which 1 were waited for; matrix products, arithmetic and copies ran while one was open for 0% of the time, Pallas kernels for 0%

profile of v4, /device:TPU:8, one launch (start us, length us, event | category | flops | bytes accessed | tf_op | source)
XLA Modules:
  0.0 88.0 jit_solution(6521414829351563977)
XLA Ops:
  0.0 0.0 copy-start.2
  0.0 0.0 copy-start.1
  0.0 0.0 copy-start
  0.0 3.6 %spectra.1 = bf16[1024,256]{1,0:T(8,128)(2,1)S(1)} custom-call(bf16[4,256,2048]{2,1,0:T(8,128)(2,1)} %img_hbm.1, bf16[2,256,2048]{2,1,0:T(8,128)(2,1)} %constant.2.clone.table_hbm), custom_call_target="tpu_custom_call" | custom-call | tf_op jit(solution)/shard_map/spectra/pallas_call | solution.py:75
  3.6 32.7 %all_to_all.15 = bf16[128,8,256]{2,1,0:T(8,128)(2,1)S(1)} all-to-all(bf16[128,8,256]{2,1,0:T(8,128)(2,1)S(1)} %bitcast.9), channel_id=1, replica_groups={{0,41,82,123,4,45,86,127,40,81,122,3,44,85,126,7,80,121,2,43,84,125,6,4..., dimensions={0} | all-to-all | bytes 1048576 | tf_op jit(solution)/shard_map/all_to_all | solution.py:213
  36.3 0.5 gram.1
  36.8 1.9 %collective-permute-start = (f32[2,64,512]{2,1,0:T(8,128)S(1)}, f32[2,64,512]{2,1,0:T(8,128)S(1)}, u32[]{:S(2)}, u32[]{:S(2)}) collective-permute-start(f32[2,64,512]{2,1,0:T(8,128)S(1)} %get-tuple-element.8), channel_id=1, source_target_pairs={{0,128},{1,129},{2,130},{3,131},{4,132},{5,133},{6,134},{7,135},{8... | collective-permute-start | bytes 786440 | tf_op jit(solution)/shard_map/ppermute | solution.py:219
  38.7 1.5 %collective-permute-done.got_ref = f32[2,64,512]{2,1,0:T(8,128)S(1)} collective-permute-done((f32[2,64,512]{2,1,0:T(8,128)S(1)}, f32[2,64,512]{2,1,0:T(8,128)S(1)}, u32[]{:S(2)}, u32[]{:S(2)}) %collective-permute-start) | collective-permute-done | bytes 262176 | tf_op jit(solution)/shard_map/ppermute | solution.py:219
  40.3 29.9 %all_to_all.16 = bf16[256,2,128]{2,1,0:T(2,128)(2,1)S(1)} all-to-all(bf16[256,2,128]{2,1,0:T(2,128)(2,1)S(1)} %bitcast.10), channel_id=1, replica_groups={{0,41,82,123,4,45,86,127,40,81,122,3,44,85,126,7,80,121,2,43,84,125,6,4..., dimensions={0} | all-to-all | bytes 262144 | tf_op jit(solution)/shard_map/all_to_all | solution.py:226
  70.2 0.0 copy-done.2
  70.2 0.0 copy-done.1
  70.2 0.3 legendre.1
  70.5 16.6 %all_to_all.17 = f32[128,1,128]{2,1,0:T(1,128)S(1)} all-to-all(f32[128,1,128]{2,1,0:T(1,128)S(1)} %bitcast.12), channel_id=1, replica_groups={{0,41,82,123,4,45,86,127,40,81,122,3,44,85,126,7,80,121,2,43,84,125,6,4..., dimensions={0} | all-to-all | bytes 131072 | tf_op jit(solution)/shard_map/all_to_all | solution.py:233
  87.1 0.0 copy-done
  87.1 0.9 project.1
  (1 shorter events, 0.0 us)
Async XLA Ops:
  0.0 70.2 %copy-start.2 = (f32[128,128]{1,0:T(8,128)S(1)}, f32[128,128]{1,0:T(8,128)}, u32[]{:S(2)}) copy-start(f32[128,128]{1,0:T(8,128)} %imag_ref.1) | copy-start | bytes 196612
  0.0 70.2 %copy-start.1 = (f32[128,128]{1,0:T(8,128)S(1)}, f32[128,128]{1,0:T(8,128)}, u32[]{:S(2)}) copy-start(f32[128,128]{1,0:T(8,128)} %real_ref.1) | copy-start | bytes 196612
  0.0 87.1 %copy-start = (f32[1,256,128]{2,1,0:T(8,128)S(1)}, f32[1,256,128]{2,1,0:T(8,128)}, u32[]{:S(2)}) copy-start(f32[1,256,128]{2,1,0:T(8,128)} %amp_ref.1) | copy-start | bytes 393220
  36.8 3.4 %collective-permute-start = (f32[2,64,512]{2,1,0:T(8,128)S(1)}, f32[2,64,512]{2,1,0:T(8,128)S(1)}, u32[]{:S(2)}, u32[]{:S(2)}) collective-permute-start(f32[2,64,512]{2,1,0:T(8,128)S(1)} %get-tuple-element.8), channel_id=1, source_target_pairs={{0,128},{1,129},{2,130},{3,131},{4,132},{5,133},{6,134},{7,135},{8... | collective-permute-start | bytes 786440 | tf_op jit(solution)/shard_map/ppermute | solution.py:219

commit v5 on v4

--- a/solution.py
+++ b/solution.py
@@ -21,13 +21,6 @@
     real, imag = np.cos(phase) * norm_scale, -np.sin(phase) * norm_scale
     both = [np.concatenate([real, imag]), np.concatenate([real[::-1], imag[::-1]])]
     return np.stack(both).astype(ml_dtypes.bfloat16)
-
-
-def skewed_order():
-    return [
-        ((z + x + y) % 4 * 4 + (x + y) % 4) * 8 + y
-        for z in range(4) for x in range(4) for y in range(8)
-    ]
 
 
 def spectra_kernel(img_hbm, table_hbm, out_ref, img_ref, table_ref, rows_ref, img_sem, table_sem):
@@ -157,15 +150,7 @@
     exact = functools.partial(
         jnp.dot, precision=lax.Precision.HIGHEST, preferred_element_type=jnp.float32
     )
-    result = exact(real_ref[...], summed(0)) + exact(imag_ref[...], summed(1))
-    tiles = result.reshape(result.shape[0] // 8, 8, LANES)
-    spot = lax.broadcasted_iota(jnp.int32, (8, LANES), 0) % 4
-    for z in range(4):
-        for x in range(4):
-            rows = tiles[z * 4 + x]
-            for y in range(4):
-                rows = jnp.where(spot == y, tiles[(z + x + y) % 4 * 4 + (x + y) % 4], rows)
-            out_ref[(z * 4 + x) * 8:(z * 4 + x + 1) * 8, :] = rows
+    out_ref[...] = exact(real_ref[...], summed(0)) + exact(imag_ref[...], summed(1))
 
 
 def legendre_call(corr, legendre_real, legendre_imag):
@@ -207,8 +192,7 @@
 
     spectra = spectra_call(images, jnp.asarray(table_rows(points, HARMS)))
     spectra = spectra.reshape(HARMS, 2 * local_img, radii)
-    order = skewed_order()
-    rings = [[g * owners + w for w in order] for g in range(groups)]
+    rings = [[g * owners + w for w in range(owners)] for g in range(groups)]
     both_ways = [ring[::-1] if g % 2 else ring for g, ring in enumerate(rings)]
     pooled = lax.all_to_all(
         spectra, ("grp", "wide"), split_axis=0, concat_axis=0, axis_index_groups=both_ways, tiled=True
@@ -220,7 +204,7 @@
     corr = merge_call(own, got, total_img)
 
     columns = [
-        [(2 * top + core) * owners + w for top in range(2) for w in order]
+        [(2 * top + core) * owners + w for top in range(2) for w in range(owners)]
         for core in range(2)
     ]
     every_harm = lax.all_to_all(

time: 88.2 us -> 87.4 us (level)
    all_to_all x1, blocking collectives: 29.9 us -> 27.4 us  [body(): lax.all_to_all(corr.reshape(2 * owners, 2, LANES), ('grp', 'wide'), split...]
    all_to_all x1, blocking collectives: 16.6 us -> 17.9 us  [body(): lax.all_to_all(degree_part.reshape(owners, 1, LANES), ('grp', 'wide'), sp...]
where the time goes in v5:
time: 87.4 us; the launch traced here: 87.1 us
  blocking collectives  78.4 us (90%)
  Pallas kernels  5.28 us (6%)
  starting transfers between devices  1.92 us (2%)
  waiting for transfers between devices  1.5 us (2%)
    all_to_all x1, blocking collectives, body(): lax.all_to_all(spectra, ('grp', 'wide'), split_axis=0, concat_axis=0, axi...  33.1 us
    all_to_all x1, blocking collectives, body(): lax.all_to_all(corr.reshape(2 * owners, 2, LANES), ('grp', 'wide'), split...  27.4 us
    all_to_all x1, blocking collectives, body(): lax.all_to_all(degree_part.reshape(owners, 1, LANES), ('grp', 'wide'), sp...  17.9 us
    pallas_call x1, Pallas kernels, spectra_call(): pl.pallas_call(spectra_kernel, out_shape=jax.ShapeDtypeStruct((rows, radi...  3.57 us
    ppermute x1, starting transfers between devices, body(): got = lax.ppermute(send, ('grp', 'wide'), swap)  1.92 us
  transfers between devices with their start and end apart: 1, of which 1 were waited for; matrix products, arithmetic and copies ran while one was open for 0% of the time, Pallas kernels for 0%

profile of v5, /device:TPU:8, one launch (start us, length us, event | category | flops | bytes accessed | tf_op | source)
XLA Modules:
  0.0 87.1 jit_solution(4196235055901089790)
XLA Ops:
  0.0 0.0 copy-start.2
  0.0 0.0 copy-start.1
  0.0 0.0 copy-start
  0.0 3.6 %spectra.1 = bf16[1024,256]{1,0:T(8,128)(2,1)S(1)} custom-call(bf16[4,256,2048]{2,1,0:T(8,128)(2,1)} %img_hbm.1, bf16[2,256,2048]{2,1,0:T(8,128)(2,1)} %constant.2.clone.table_hbm), custom_call_target="tpu_custom_call" | custom-call | tf_op jit(solution)/shard_map/spectra/pallas_call | solution.py:68
  3.6 33.1 %all_to_all.15 = bf16[128,8,256]{2,1,0:T(8,128)(2,1)S(1)} all-to-all(bf16[128,8,256]{2,1,0:T(8,128)(2,1)S(1)} %bitcast.9), channel_id=1, replica_groups={{0,1,2,3,4,5,6,7,8,9,10,11,12,13,14,15,16,17,18,19,20,21,22,23,24,25,26..., dimensions={0} | all-to-all | bytes 1048576 | tf_op jit(solution)/shard_map/all_to_all | solution.py:197
  36.7 0.5 gram.1
  37.2 1.9 %collective-permute-start = (f32[2,64,512]{2,1,0:T(8,128)S(1)}, f32[2,64,512]{2,1,0:T(8,128)S(1)}, u32[]{:S(2)}, u32[]{:S(2)}) collective-permute-start(f32[2,64,512]{2,1,0:T(8,128)S(1)} %get-tuple-element.8), channel_id=1, source_target_pairs={{0,128},{1,129},{2,130},{3,131},{4,132},{5,133},{6,134},{7,135},{8... | collective-permute-start | bytes 786440 | tf_op jit(solution)/shard_map/ppermute | solution.py:203
  39.1 1.5 %collective-permute-done.got_ref = f32[2,64,512]{2,1,0:T(8,128)S(1)} collective-permute-done((f32[2,64,512]{2,1,0:T(8,128)S(1)}, f32[2,64,512]{2,1,0:T(8,128)S(1)}, u32[]{:S(2)}, u32[]{:S(2)}) %collective-permute-start) | collective-permute-done | bytes 262176 | tf_op jit(solution)/shard_map/ppermute | solution.py:203
  40.7 27.4 %all_to_all.16 = bf16[256,2,128]{2,1,0:T(2,128)(2,1)S(1)} all-to-all(bf16[256,2,128]{2,1,0:T(2,128)(2,1)S(1)} %bitcast.10), channel_id=1, replica_groups={{0,1,2,3,4,5,6,7,8,9,10,11,12,13,14,15,16,17,18,19,20,21,22,23,24,25,26..., dimensions={0} | all-to-all | bytes 262144 | tf_op jit(solution)/shard_map/all_to_all | solution.py:210
  68.1 0.0 copy-done.2
  68.1 0.0 copy-done.1
  68.1 0.3 legendre.1
  68.4 17.9 %all_to_all.17 = f32[128,1,128]{2,1,0:T(1,128)S(1)} all-to-all(f32[128,1,128]{2,1,0:T(1,128)S(1)} %bitcast.12), channel_id=1, replica_groups={{0,1,2,3,4,5,6,7,8,9,10,11,12,13,14,15,16,17,18,19,20,21,22,23,24,25,26..., dimensions={0} | all-to-all | bytes 131072 | tf_op jit(solution)/shard_map/all_to_all | solution.py:217
  86.3 0.0 copy-done
  86.3 0.9 project.1
  (1 shorter events, 0.0 us)
Async XLA Ops:
  0.0 68.1 %copy-start.2 = (f32[128,128]{1,0:T(8,128)S(1)}, f32[128,128]{1,0:T(8,128)}, u32[]{:S(2)}) copy-start(f32[128,128]{1,0:T(8,128)} %imag_ref.1) | copy-start | bytes 196612
  0.0 68.1 %copy-start.1 = (f32[128,128]{1,0:T(8,128)S(1)}, f32[128,128]{1,0:T(8,128)}, u32[]{:S(2)}) copy-start(f32[128,128]{1,0:T(8,128)} %real_ref.1) | copy-start | bytes 196612
  0.0 86.3 %copy-start = (f32[1,256,128]{2,1,0:T(8,128)S(1)}, f32[1,256,128]{2,1,0:T(8,128)}, u32[]{:S(2)}) copy-start(f32[1,256,128]{2,1,0:T(8,128)} %amp_ref.1) | copy-start | bytes 393220
  37.2 3.4 %collective-permute-start = (f32[2,64,512]{2,1,0:T(8,128)S(1)}, f32[2,64,512]{2,1,0:T(8,128)S(1)}, u32[]{:S(2)}, u32[]{:S(2)}) collective-permute-start(f32[2,64,512]{2,1,0:T(8,128)S(1)} %get-tuple-element.8), channel_id=1, source_target_pairs={{0,128},{1,129},{2,130},{3,131},{4,132},{5,133},{6,134},{7,135},{8... | collective-permute-start | bytes 786440 | tf_op jit(solution)/shard_map/ppermute | solution.py:203

commit v6 on v5

--- a/solution.py
+++ b/solution.py
@@ -19,7 +19,7 @@
     phase = product.astype(np.float32) * np.float32(2.0 * math.pi / points)
     norm_scale = np.float32(1.0 / math.sqrt(points))
     real, imag = np.cos(phase) * norm_scale, -np.sin(phase) * norm_scale
-    both = [np.concatenate([real, imag]), np.concatenate([real[::-1], imag[::-1]])]
+    both = [np.concatenate([real[::-1], imag[::-1]]), np.concatenate([real, imag])]
     return np.stack(both).astype(ml_dtypes.bfloat16)
 
 
@@ -193,7 +193,7 @@
     spectra = spectra_call(images, jnp.asarray(table_rows(points, HARMS)))
     spectra = spectra.reshape(HARMS, 2 * local_img, radii)
     rings = [[g * owners + w for w in range(owners)] for g in range(groups)]
-    both_ways = [ring[::-1] if g % 2 else ring for g, ring in enumerate(rings)]
+    both_ways = [ring if g % 2 else ring[::-1] for g, ring in enumerate(rings)]
     pooled = lax.all_to_all(
         spectra, ("grp", "wide"), split_axis=0, concat_axis=0, axis_index_groups=both_ways, tiled=True
     )

time: 87.4 us -> 87.8 us (level)
  the two profiles are of different devices: /device:TPU:8 before, /device:TPU:2 now
where the time goes in v6:
time: 87.8 us; the launch traced here: 87.6 us
  blocking collectives  78.8 us (90%)
  Pallas kernels  5.28 us (6%)
  starting transfers between devices  1.92 us (2%)
  waiting for transfers between devices  1.5 us (2%)
    all_to_all x1, blocking collectives, body(): lax.all_to_all(spectra, ('grp', 'wide'), split_axis=0, concat_axis=0, axi...  32.2 us
    all_to_all x1, blocking collectives, body(): lax.all_to_all(corr.reshape(2 * owners, 2, LANES), ('grp', 'wide'), split...  28.6 us
    all_to_all x1, blocking collectives, body(): lax.all_to_all(degree_part.reshape(owners, 1, LANES), ('grp', 'wide'), sp...  18.1 us
    pallas_call x1, Pallas kernels, spectra_call(): pl.pallas_call(spectra_kernel, out_shape=jax.ShapeDtypeStruct((rows, radi...  3.57 us
    ppermute x1, starting transfers between devices, body(): got = lax.ppermute(send, ('grp', 'wide'), swap)  1.92 us
  transfers between devices with their start and end apart: 1, of which 1 were waited for; matrix products, arithmetic and copies ran while one was open for 0% of the time, Pallas kernels for 0%

profile of v6, /device:TPU:2, one launch (start us, length us, event | category | flops | bytes accessed | tf_op | source)
XLA Modules:
  0.0 87.6 jit_solution(2317491013795829131)
XLA Ops:
  0.0 0.0 copy-start.2
  0.0 0.0 copy-start.1
  0.0 0.0 copy-start
  0.0 3.6 %spectra.1 = bf16[1024,256]{1,0:T(8,128)(2,1)S(1)} custom-call(bf16[4,256,2048]{2,1,0:T(8,128)(2,1)} %img_hbm.1, bf16[2,256,2048]{2,1,0:T(8,128)(2,1)} %constant.2.clone.table_hbm), custom_call_target="tpu_custom_call" | custom-call | tf_op jit(solution)/shard_map/spectra/pallas_call | solution.py:68
  3.6 32.2 %all_to_all.15 = bf16[128,8,256]{2,1,0:T(8,128)(2,1)S(1)} all-to-all(bf16[128,8,256]{2,1,0:T(8,128)(2,1)S(1)} %bitcast.9), channel_id=1, replica_groups={{127,126,125,124,123,122,121,120,119,118,117,116,115,114,113,112,111,11..., dimensions={0} | all-to-all | bytes 1048576 | tf_op jit(solution)/shard_map/all_to_all | solution.py:197
  35.8 0.5 gram.1
  36.3 1.9 %collective-permute-start = (f32[2,64,512]{2,1,0:T(8,128)S(1)}, f32[2,64,512]{2,1,0:T(8,128)S(1)}, u32[]{:S(2)}, u32[]{:S(2)}) collective-permute-start(f32[2,64,512]{2,1,0:T(8,128)S(1)} %get-tuple-element.8), channel_id=1, source_target_pairs={{0,128},{1,129},{2,130},{3,131},{4,132},{5,133},{6,134},{7,135},{8... | collective-permute-start | bytes 786440 | tf_op jit(solution)/shard_map/ppermute | solution.py:203
  38.2 1.5 %collective-permute-done.got_ref = f32[2,64,512]{2,1,0:T(8,128)S(1)} collective-permute-done((f32[2,64,512]{2,1,0:T(8,128)S(1)}, f32[2,64,512]{2,1,0:T(8,128)S(1)}, u32[]{:S(2)}, u32[]{:S(2)}) %collective-permute-start) | collective-permute-done | bytes 262176 | tf_op jit(solution)/shard_map/ppermute | solution.py:203
  39.8 28.6 %all_to_all.16 = bf16[256,2,128]{2,1,0:T(2,128)(2,1)S(1)} all-to-all(bf16[256,2,128]{2,1,0:T(2,128)(2,1)S(1)} %bitcast.10), channel_id=1, replica_groups={{0,1,2,3,4,5,6,7,8,9,10,11,12,13,14,15,16,17,18,19,20,21,22,23,24,25,26..., dimensions={0} | all-to-all | bytes 262144 | tf_op jit(solution)/shard_map/all_to_all | solution.py:210
  68.3 0.0 copy-done.2
  68.3 0.0 copy-done.1
  68.3 0.3 legendre.1
  68.6 18.1 %all_to_all.17 = f32[128,1,128]{2,1,0:T(1,128)S(1)} all-to-all(f32[128,1,128]{2,1,0:T(1,128)S(1)} %bitcast.12), channel_id=1, replica_groups={{0,1,2,3,4,5,6,7,8,9,10,11,12,13,14,15,16,17,18,19,20,21,22,23,24,25,26..., dimensions={0} | all-to-all | bytes 131072 | tf_op jit(solution)/shard_map/all_to_all | solution.py:217
  86.7 0.0 copy-done
  86.7 0.9 project.1
  (1 shorter events, 0.0 us)
Async XLA Ops:
  0.0 68.3 %copy-start.2 = (f32[128,128]{1,0:T(8,128)S(1)}, f32[128,128]{1,0:T(8,128)}, u32[]{:S(2)}) copy-start(f32[128,128]{1,0:T(8,128)} %imag_ref.1) | copy-start | bytes 196612
  0.0 68.3 %copy-start.1 = (f32[128,128]{1,0:T(8,128)S(1)}, f32[128,128]{1,0:T(8,128)}, u32[]{:S(2)}) copy-start(f32[128,128]{1,0:T(8,128)} %real_ref.1) | copy-start | bytes 196612
  0.0 86.7 %copy-start = (f32[1,256,128]{2,1,0:T(8,128)S(1)}, f32[1,256,128]{2,1,0:T(8,128)}, u32[]{:S(2)}) copy-start(f32[1,256,128]{2,1,0:T(8,128)} %amp_ref.1) | copy-start | bytes 393220
  36.3 3.4 %collective-permute-start = (f32[2,64,512]{2,1,0:T(8,128)S(1)}, f32[2,64,512]{2,1,0:T(8,128)S(1)}, u32[]{:S(2)}, u32[]{:S(2)}) collective-permute-start(f32[2,64,512]{2,1,0:T(8,128)S(1)} %get-tuple-element.8), channel_id=1, source_target_pairs={{0,128},{1,129},{2,130},{3,131},{4,132},{5,133},{6,134},{7,135},{8... | collective-permute-start | bytes 786440 | tf_op jit(solution)/shard_map/ppermute | solution.py:203
